TPU v7x, 32 devices: a whole 2x2x4 slice. The times are simulated.
32 devices in a mesh: grp: 8 (over z, core), tp: 4 (over y, x).
Axes of the slice: x: 2, y: 2, z: 4, core: 2. Of those that a mesh axis runs over, the one named last changes fastest.
Arguments:
- hidden: bfloat16 [128, 16384], P(('grp', 'tp')), may hold values from -130 to 130
- gain: float32 [16384], replicated, may hold values from 0.5 to 1.5
- head: bfloat16 [16384, 16384], P(None, ('grp', 'tp')), may hold values from -3 to 3
Outputs:
- log_probs: float32 [128, 16384], P(('grp', 'tp'))
All inputs are finite; a program needn't handle non-finite values.
Results may differ from a plain program's by a relative error of at most 0.00055.
Values may be sent and summed in bfloat16 or wider, within the bound.
No kernel may reach another device: no remote copies, remote signals or barrier semaphores. Data moves between devices by JAX's collectives and lax.ppermute only.
A program may use at most 128 MiB of HBM per device.

v0:
```python
import jax
import jax.numpy as jnp
from jax import lax
from jax.sharding import PartitionSpec as P


def on_device(hidden, gain, head):
    values = hidden.astype(jnp.float32)
    mean_square = jnp.mean(values * values, axis=-1, keepdims=True)
    normed = (values * lax.rsqrt(mean_square + 1e-05) * gain).astype(jnp.bfloat16)
    group_block = lax.all_gather(normed, "tp", axis=0, tiled=True)
    logits = jnp.dot(
        lax.all_gather(group_block, "grp", axis=0, tiled=True),
        head,
        preferred_element_type=jnp.float32,
    )
    owned = lax.all_to_all(logits, ("grp", "tp"), split_axis=0, concat_axis=1, tiled=True)
    top = jnp.max(owned, axis=-1, keepdims=True)
    total = jnp.sum(jnp.exp(owned - top), axis=-1, keepdims=True)
    return owned - top - jnp.log(total)


def solution(mesh):
    return jax.shard_map(
        on_device,
        mesh=mesh,
        in_specs=(P(("grp", "tp"), None), P(), P(None, ("grp", "tp"))),
        out_specs=P(("grp", "tp"), None),
        check_vma=False,
    )
```

profile of v0, /device:TPU:0, one launch (start us, length us, event | category | flops | bytes accessed | tf_op | source)
XLA Modules:
  0.0 100.4 jit_solution(16595028020233734949)
XLA Ops:
  6.5 0.0 all-gather.3.cloned.1.call-start
  6.5 1.2 %fusion = f32[4]{0:T(128)S(1)} fusion(bf16[4,16384]{1,0:T(4,128)(2,1)} %param.3), kind=kLoop, calls=%fused_computation.2 | loop fusion | flops 196604 | bytes 131088 | tf_op jit(solution)/shard_map/reduce_sum | solution.py:9
  7.7 1.0 %fusion.5 = bf16[1,4,16384]{2,1,0:T(4,128)(2,1)S(1)} fusion(bf16[4,16384]{1,0:T(4,128)(2,1)} %param.3, f32[16384]{0:T(1024)} %param.4, f32[4]{0:T(128)S(1)} %add_rsqrt_fusion), kind=kLoop, calls=%fused_computation.9 | loop fusion | flops 262144 | bytes 327696
  8.7 11.5 %all-gather = bf16[4,4,16384]{2,1,0:T(4,128)(2,1)S(1)} all-gather(bf16[1,4,16384]{2,1,0:T(4,128)(2,1)S(1)} %fusion.5), channel_id=1, replica_groups=mesh['grp'=8,'tp'=4] {'tp'}, dimensions={0}, use_global_device_ids=true | all-gather | bytes 655360 | tf_op jit(solution)/shard_map/all_gather | solution.py:11
  20.3 0.9 reshape.22
  21.2 0.0 all-gather.3.cloned.1.call-update
  21.2 47.3 %all-gather.3.cloned.1.call-done = bf16[128,16384]{1,0:T(8,128)(2,1)} async-done(((bf16[16,16384]{1,0:T(8,128)(2,1)}), bf16[128,16384]{1,0:T(8,128)(2,1)}) %all-gather.3.cloned.1.call-update) | async-done | bytes 4194320 | tf_op jit(solution)/shard_map/all_gather | solution.py:13
  68.5 9.4 %fusion.6 = f32[128,512]{1,0:T(8,128)S(1)} fusion(bf16[128,16384]{1,0:T(8,128)(2,1)} %all-gather.3.cloned.1.call-done, bf16[16384,512]{1,0:T(8,128)(2,1)} %param.5), kind=kOutput, calls=%fused_computation.11 | convolution fusion | flops 2147483648 | bytes 21233664 | tf_op jit(solution)/shard_map/dot_general | solution.py:12
  77.9 0.1 all_to_all.14
  78.0 14.1 %all_to_all.19 = f32[32,4,512]{2,1,0:T(4,128)S(1)} all-to-all(f32[32,4,512]{2,1,0:T(4,128)S(1)} %all_to_all.14), channel_id=1, replica_groups=mesh['grp'=8,'tp'=4] {'grp','tp'}, dimensions={0} | all-to-all | bytes 524288 | tf_op jit(solution)/shard_map/all_to_all | solution.py:17
  92.1 0.3 reduce_max.9
  92.4 0.3 fusion.4
  92.7 0.8 subtract_subtract_fusion
  (2 shorter events, 0.0 us)
Async XLA Ops:
  6.5 62.0 %all-gather.3.cloned.1.call-start = ((), (), s32[]{:S(2)}) async-start(), calls=%async_computation.1 | async-start | bytes 4718592 | tf_op jit(solution)/shard_map/all_gather | solution.py:13
Sparse Core Ops, SparseCore 0:
  21.3 47.1 all-gather.2
where the time goes:
time: 101 us; the launch traced here: 100 us
  waiting for transfers between devices  47.3 us (47%)
  blocking collectives  25.7 us (25%)
  between operations  13.4 us (13%)
  matrix products  9.38 us (9%)
  other arithmetic  3.61 us (4%)
    all_gather x1, waiting for transfers between devices, on_device(): lax.all_gather(group_block, 'grp', axis=0, tiled=True)  47.3 us
    all_to_all x1, blocking collectives, on_device(): lax.all_to_all(logits, ('grp', 'tp'), split_axis=0, concat_axis=1, tiled=...  14.1 us
    all_gather x1, blocking collectives, on_device(): group_block = lax.all_gather(normed, 'tp', axis=0, tiled=True)  11.5 us
    dot_general x1, matrix products, on_device(): jnp.dot(lax.all_gather(group_block, 'grp', axis=0, tiled=True), head, pre...  9.38 us
  transfers between devices with their start and end apart: 1, of which 1 were waited for; matrix products, arithmetic and copies ran while one was open for 0% of the time, Pallas kernels for 0%

commit v1 on v0

v1 whole, which is shorter than its diff:
```python
import jax
import jax.numpy as jnp
from jax import lax
from jax.experimental import pallas as pl
from jax.experimental.pallas import tpu as pltpu
from jax.sharding import PartitionSpec as P


AXES = ("grp", "tp")
EPS = 1e-05
PAD = 128
SCALE = 0.25
VMEM = pltpu.VMEM


def bits_between(low, high):
    bits = []
    while low < high:
        bits.append(low)
        low *= 2
    assert low == high
    return bits


def interleave(a, b):
    mixed = []
    for i in range(max(len(a), len(b))):
        mixed += a[i : i + 1] + b[i : i + 1]
    return mixed


def plan(groups, tp):
    near = bits_between(1, tp)
    far = bits_between(2 * tp, groups * tp)[::-1]
    back = near[::-1]
    return [
        (10, (far + near, far + back)),
        (6, (interleave(near, far), interleave(back, far))),
    ]


def vmem_spec():
    return pl.BlockSpec(memory_space=VMEM)


def in_vmem(x):
    return pltpu.with_memory_space_constraint(x, VMEM)


def in_hbm(x):
    return pltpu.with_memory_space_constraint(x, pltpu.HBM)


def norm_kernel(own_ref, other_ref, gain_ref, *out_refs):
    width = own_ref.shape[1]
    core = lax.rem(lax.axis_index("grp"), 2)
    half = width // 2
    own, other = own_ref[...].astype(jnp.float32), other_ref[...].astype(jnp.float32)
    mine = core == 0
    values = jnp.concatenate([jnp.where(mine, own, other), jnp.where(mine, other, own)], axis=0)
    mean_square = jnp.mean(values * values, axis=-1, keepdims=True)
    scale = lax.rsqrt(mean_square + EPS)
    start = 0
    for out_ref in out_refs:
        span = out_ref.shape[1]
        columns = pl.ds(pl.multiple_of(core * half + start, 128), span)
        part = jnp.where(mine, values[:, start : start + span], values[:, half + start : half + start + span])
        out_ref[...] = (part * scale * gain_ref[:, columns]).astype(jnp.bfloat16)
        start += span


def prep_kernel(hidden_ref, gain_ref, hidden_out, gain_out, sems):
    copies = [
        pltpu.make_async_copy(hidden_ref, hidden_out, sems.at[0]),
        pltpu.make_async_copy(gain_ref, gain_out, sems.at[1]),
    ]
    for copy in copies:
        copy.start()
    for copy in copies:
        copy.wait()


def prep(hidden, gain):
    gain = gain.reshape(1, -1)
    return pl.pallas_call(
        prep_kernel,
        out_shape=[jax.ShapeDtypeStruct(x.shape, x.dtype) for x in (hidden, gain)],
        in_specs=[pl.BlockSpec(memory_space=pltpu.HBM)] * 2,
        out_specs=[vmem_spec()] * 2,
        scratch_shapes=[pltpu.SemaphoreType.DMA((2,))],
        compiler_params=pltpu.CompilerParams(vmem_limit_bytes=2 << 20),
        cost_estimate=pl.CostEstimate(flops=0, bytes_accessed=4 * hidden.size, transcendentals=0),
        name="prep",
    )(in_hbm(hidden), in_hbm(gain))


def norm(hidden, other, gain, widths):
    tokens = hidden.shape[0]
    return pl.pallas_call(
        norm_kernel,
        out_shape=[jax.ShapeDtypeStruct((2 * tokens, w), jnp.bfloat16) for w in widths],
        in_specs=[vmem_spec()] * 3,
        out_specs=[vmem_spec()] * len(widths),
        compiler_params=pltpu.CompilerParams(vmem_limit_bytes=6 << 20),
        cost_estimate=pl.CostEstimate(flops=10 * hidden.size, bytes_accessed=4 * hidden.size, transcendentals=0),
        name="norm",
    )(hidden, other, gain)


def chip_offsets(bits, count):
    offsets = []
    for r in range(count):
        offset = 0
        for s, bit in enumerate(bits):
            if (r >> s) & 1:
                offset = offset ^ bit
        offsets.append(offset)
    return offsets


def add_blocks(tp, acc_ref, total, offsets, k_core, fresh):
    grp, t = lax.axis_index("grp"), lax.axis_index("tp")
    here = (grp - lax.rem(grp, 2)) * tp + t
    block = acc_ref.shape[1]
    for r, (off0, off1) in enumerate(offsets):
        chip = here ^ (off0 if off0 == off1 else off0 + k_core * (off1 - off0))
        slot = (chip // (2 * tp)) * tp + chip % tp
        value = total[r * block : (r + 1) * block, :]
        if fresh:
            acc_ref[slot] = value
        else:
            acc_ref[slot] += value


def head_kernel(tp, terms, last, fresh, *refs):
    refs = list(refs)
    pieces = refs[: len(terms)]
    head_ref = refs[len(terms)]
    if last:
        acc_in, out_ref, acc_ref = refs[len(terms) + 1 :]
        acc_ref[...] = acc_in[...]
    else:
        acc_ref = refs[-1]
    core = lax.rem(lax.axis_index("grp"), 2)
    half = head_ref.shape[0] // 2
    if fresh:
        acc_ref[...] = jnp.zeros_like(acc_ref)
    for ref, (start, offsets, own) in zip(pieces, terms):
        k_core = core if own else 1 - core
        span = ref.shape[1]
        step = min(span, 1024)
        while span % step:
            step //= 2
        total = None
        for k in range(0, span, step):
            rows = pl.ds(pl.multiple_of(k_core * half + start + k, 128), step)
            part = jnp.dot(ref[:, k : k + step], head_ref[rows, :], preferred_element_type=jnp.float32)
            total = part if total is None else total + part
        add_blocks(tp, acc_ref, total, offsets, k_core, False)
    if last:
        chips, block, width = acc_ref.shape
        tokens = block // 2
        for q in range(chips):
            logits = acc_ref[q]
            top = jnp.max(logits, axis=-1, keepdims=True)
            lse = top + jnp.log(jnp.sum(jnp.exp(logits - top), axis=-1, keepdims=True))
            sent = (logits - lse) * SCALE
            scaled = lse * SCALE
            high = jnp.floor(scaled / 16 + 0.5) * 16
            mid = jnp.floor((scaled - high) * 64 + 0.5) / 64
            low = scaled - high - mid
            lane = lax.broadcasted_iota(jnp.int32, (block, PAD), 1)
            tail = jnp.where(lane == 0, high, jnp.where(lane == 1, mid, low))
            d = (q // tp) * 2 * tp + q % tp
            for c in range(2):
                out_ref[d + c * tp, :, :width] = sent[c * tokens : (c + 1) * tokens]
                out_ref[d + c * tp, :, width:] = tail[c * tokens : (c + 1) * tokens]


def head_part(tp, chips, block, pieces, terms, head, acc, last=False):
    width = head.shape[1]
    acc_shape = (chips, block, width)
    fresh = acc is None
    args = [in_vmem(p) for p in pieces] + [head] + ([] if fresh else [acc])

    def kernel(*refs):
        head_kernel(tp, terms, last, fresh, *refs)

    if last:
        out = jax.ShapeDtypeStruct((2 * chips, block // 2, width + PAD), jnp.float32)
    else:
        out = jax.ShapeDtypeStruct(acc_shape, jnp.float32)
    work = sum(p.size for p in pieces)
    return pl.pallas_call(
        kernel,
        out_shape=out,
        in_specs=[vmem_spec()] * len(args),
        out_specs=vmem_spec(),
        scratch_shapes=[VMEM(acc_shape, jnp.float32)] if last else [],
        input_output_aliases={} if fresh or last else {len(args) - 1: 0},
        compiler_params=pltpu.CompilerParams(vmem_limit_bytes=8 << 20),
        cost_estimate=pl.CostEstimate(flops=2 * work * width, bytes_accessed=2 * work, transcendentals=0),
        name="head",
    )(*args)


def load_kernel(head_ref, out_ref, sem):
    copy = pltpu.make_async_copy(head_ref, out_ref, sem)
    copy.start()
    copy.wait()


def load(head):
    return pl.pallas_call(
        load_kernel,
        out_shape=jax.ShapeDtypeStruct(head.shape, head.dtype),
        in_specs=[pl.BlockSpec(memory_space=pltpu.HBM)],
        out_specs=vmem_spec(),
        scratch_shapes=[pltpu.SemaphoreType.DMA],
        compiler_params=pltpu.CompilerParams(vmem_limit_bytes=2 << 20),
        cost_estimate=pl.CostEstimate(flops=0, bytes_accessed=2 * head.size, transcendentals=0),
        name="load",
    )(in_hbm(head))


def finish_kernel(got_ref, out_ref):
    devices, _, wide = got_ref.shape
    width = wide - PAD
    parts = got_ref[:, :, width : width + PAD]
    lse = (parts[:, :, 0:1] + parts[:, :, 1:2] + parts[:, :, 2:3]) / SCALE
    top = jnp.max(lse, axis=0, keepdims=True)
    whole = top + jnp.log(jnp.sum(jnp.exp(lse - top), axis=0, keepdims=True))
    shift = lse - whole
    for d in range(devices):
        out_ref[:, d * width : (d + 1) * width] = got_ref[d, :, :width] / SCALE + shift[d]


def finish(got, width):
    devices, tokens, _ = got.shape
    return pl.pallas_call(
        finish_kernel,
        out_shape=jax.ShapeDtypeStruct((tokens, devices * width), jnp.float32),
        in_specs=[vmem_spec()],
        out_specs=vmem_spec(),
        compiler_params=pltpu.CompilerParams(vmem_limit_bytes=8 << 20),
        name="finish",
    )(got)


def solution(mesh):
    groups, tp = mesh.shape["grp"], mesh.shape["tp"]
    devices = groups * tp
    pair = [(i, i ^ tp) for i in range(devices)]

    def stage(bit0, bit1):
        return [(i, i ^ (bit1 if i & tp else bit0)) for i in range(devices)]

    chunks = plan(groups, tp)
    count = len(chunks[0][1][0])
    chips = devices // 2
    offsets = [list(zip(*(chip_offsets(o, chips) for o in orders))) for _, orders in chunks]
    near = [o[: chips // 2] for o in offsets]
    far = [o[chips // 2 :] for o in offsets]
    every = range(len(chunks))
    final = len(chunks) - 1

    def permute(x, pairs):
        return lax.ppermute(x, AXES, pairs)

    def on_device(hidden, gain, head):
        half = hidden.shape[1] // 2
        block = 2 * hidden.shape[0]
        widths = [share * half // 16 for share, _ in chunks]
        starts = [sum(widths[:j]) for j in every]
        head_here = load(head)
        other = permute(hidden, pair)
        hidden, gain = prep(hidden, gain)
        bufs = list(norm(hidden, other, gain, widths))
        recvs = [None] * len(chunks)
        for s in range(count):
            for j, (_, orders) in enumerate(chunks):
                recvs[j] = permute(bufs[j], stage(orders[0][s], orders[1][s]))
            if s < count - 1:
                for j in every:
                    bufs[j] = jnp.concatenate([bufs[j], recvs[j]], axis=0)

        def part(pieces, terms, acc, last=False):
            return head_part(tp, chips, block, pieces, terms, head_here, acc, last)

        acc = None
        for j in every:
            pieces = [bufs[j], permute(bufs[j], pair)]
            acc = part(pieces, [(starts[j], near[j], True), (starts[j], near[j], False)], acc)
        mirrored = [permute(recvs[j], pair) for j in every]
        for j in every:
            acc = part([recvs[j]], [(starts[j], far[j], True)], acc)
        for j in every:
            acc = part([mirrored[j]], [(starts[j], far[j], False)], acc, last=j == final)
        got = lax.all_to_all(acc.astype(jnp.float16), AXES, split_axis=0, concat_axis=0, tiled=True)
        return finish(got.astype(jnp.float32), head.shape[1])

    return jax.shard_map(
        on_device,
        mesh=mesh,
        in_specs=(P(AXES, None), P(), P(None, AXES)),
        out_specs=P(AXES, None),
        check_vma=False,
    )
```

time: 101 us -> 66.4 us (0.66)
  waiting for transfers between devices: 47.3 us -> 23.7 us
  Pallas kernels: 0 us -> 15 us
  between operations: 13.4 us -> 0.15 us
  starting transfers between devices: 0.01 us -> 13.1 us
  blocking collectives: 25.7 us -> 13.9 us
  matrix products: 9.38 us -> 0 us
  other arithmetic: 3.61 us -> 0.17 us
    all_gather x1 -> x0, waiting for transfers between devices: 47.3 us -> none  [on_device(): lax.all_gather(group_block, 'grp', axis=0, tiled=True)]
    ppermute x0 -> x13, waiting for transfers between devices: none -> 23.7 us  [permute(): return lax.ppermute(x, AXES, pairs)]
    pallas_call x0 -> x10, Pallas kernels: none -> 15 us  [the longest x6 6.95 us: head_part(): pl.pallas_call(kernel, out_shape=out, in_specs=[vmem_spec()] * len(args),...]
    ppermute x0 -> x13, starting transfers between devices: none -> 13.1 us  [permute(): return lax.ppermute(x, AXES, pairs)]
    all_gather x1 -> x0, blocking collectives: 11.5 us -> none  [on_device(): group_block = lax.all_gather(normed, 'tp', axis=0, tiled=True)]
    dot_general x1 -> x0, matrix products: 9.38 us -> none  [on_device(): jnp.dot(lax.all_gather(group_block, 'grp', axis=0, tiled=True), head, pre...]
    reduce_sum x2 -> x0, other arithmetic: 1.48 us -> none  [the longest x1 1.15 us: on_device(): mean_square = jnp.mean(values * values, axis=-1, keepdims=True)]
    unnamed x1 -> x0, other arithmetic: 1.05 us -> none
  transfers between devices with their start and end apart: 1 -> 13, of which waited for: 1 -> 8; matrix products, arithmetic and copies ran while one was open for 0% -> 0% of each run, Pallas kernels for 0% -> 19%
where the time goes in v1:
time: 66.4 us; the launch traced here: 66.2 us
  waiting for transfers between devices  23.7 us (36%)
  Pallas kernels  15 us (23%)
  blocking collectives  13.9 us (21%)
  starting transfers between devices  13.1 us (20%)
    ppermute x13, waiting for transfers between devices, permute(): return lax.ppermute(x, AXES, pairs)  23.7 us
    all_to_all x1, blocking collectives, on_device(): lax.all_to_all(acc.astype(jnp.float16), AXES, split_axis=0, concat_axis=0...  13.9 us
    ppermute x13, starting transfers between devices, permute(): return lax.ppermute(x, AXES, pairs)  13.1 us
    pallas_call x6, Pallas kernels, head_part(): pl.pallas_call(kernel, out_shape=out, in_specs=[vmem_spec()] * len(args),...  6.95 us
    pallas_call x1, Pallas kernels, load(): pl.pallas_call(load_kernel, out_shape=jax.ShapeDtypeStruct(head.shape, he...  5.78 us
  transfers between devices with their start and end apart: 13, of which 8 were waited for; matrix products, arithmetic and copies ran while one was open for 0% of the time, Pallas kernels for 19%

profile of v1, /device:TPU:0, one launch (start us, length us, event | category | flops | bytes accessed | tf_op | source)
XLA Modules:
  0.0 66.2 jit_solution(10149124440703663305)
XLA Ops:
  0.0 0.5 collective-permute-start
  0.5 0.9 %prep.1 = (bf16[4,16384]{1,0:T(4,128)(2,1)S(1)}, f32[1,16384]{1,0:T(1,128)S(1)}) custom-call(bf16[4,16384]{1,0:T(4,128)(2,1)} %hidden_ref.1, f32[1,16384]{1,0:T(1,128)} %bitcast.1), custom_call_target="tpu_custom_call" | custom-call | bytes 262144 | tf_op jit(solution)/shard_map/prep/pallas_call | solution.py:85
  2.0 4.0 %collective-permute-start.6 = (bf16[8,5120]{1,0:T(8,128)(2,1)S(1)}, bf16[8,5120]{1,0:T(8,128)(2,1)S(1)}, u32[]{:S(2)}, u32[]{:S(2)}) collective-permute-start(bf16[8,5120]{1,0:T(8,128)(2,1)S(1)} %get-tuple-element.12), channel_id=1, source_target_pairs={{0,16},{1,17},{2,18},{3,19},{4,20},{5,21},{6,22},{7,23},{8,24},{9,... | collective-permute-start | bytes 245768 | tf_op jit(solution)/shard_map/ppermute | solution.py:268
  6.0 1.5 %collective-permute-start.1 = (bf16[8,3072]{1,0:T(8,128)(2,1)S(1)}, bf16[8,3072]{1,0:T(8,128)(2,1)S(1)}, u32[]{:S(2)}, u32[]{:S(2)}) collective-permute-start(bf16[8,3072]{1,0:T(8,128)(2,1)S(1)} %get-tuple-element.11), channel_id=1, source_target_pairs={{0,1},{1,0},{2,3},{3,2},{4,6},{5,7},{6,4},{7,5},{8,9},{9,8},{10,11... | collective-permute-start | bytes 147464 | tf_op jit(solution)/shard_map/ppermute | solution.py:268
  7.5 2.6 %collective-permute-done.1 = bf16[8,3072]{1,0:T(8,128)(2,1)S(1)} collective-permute-done((bf16[8,3072]{1,0:T(8,128)(2,1)S(1)}, bf16[8,3072]{1,0:T(8,128)(2,1)S(1)}, u32[]{:S(2)}, u32[]{:S(2)}) %collective-permute-start.1) | collective-permute-done | bytes 49184 | tf_op jit(solution)/shard_map/ppermute | solution.py:268
  10.6 1.6 %collective-permute-start.7 = (bf16[16,5120]{1,0:T(8,128)(2,1)S(1)}, bf16[16,5120]{1,0:T(8,128)(2,1)S(1)}, u32[]{:S(2)}, u32[]{:S(2)}) collective-permute-start(bf16[16,5120]{1,0:T(8,128)(2,1)S(1)} %pad_maximum_fusion.2), channel_id=1, source_target_pairs={{0,8},{1,9},{2,10},{3,11},{4,12},{5,13},{6,14},{7,15},{8,0},{9,1},... | collective-permute-start | bytes 491528 | tf_op jit(solution)/shard_map/ppermute | solution.py:268
  12.2 4.3 %collective-permute-done.2 = bf16[16,3072]{1,0:T(8,128)(2,1)S(1)} collective-permute-done((bf16[16,3072]{1,0:T(8,128)(2,1)S(1)}, bf16[16,3072]{1,0:T(8,128)(2,1)S(1)}, u32[]{:S(2)}, u32[]{:S(2)}) %collective-permute-start.2) | collective-permute-done | bytes 98336 | tf_op jit(solution)/shard_map/ppermute | solution.py:268
  16.5 1.6 %collective-permute-start.3 = (bf16[32,3072]{1,0:T(8,128)(2,1)S(1)}, bf16[32,3072]{1,0:T(8,128)(2,1)S(1)}, u32[]{:S(2)}, u32[]{:S(2)}) collective-permute-start(bf16[32,3072]{1,0:T(8,128)(2,1)S(1)} %pad_maximum_fusion.1), channel_id=1, source_target_pairs={{0,2},{1,3},{2,0},{3,1},{4,5},{5,4},{6,7},{7,6},{8,10},{9,11},{10,... | collective-permute-start | bytes 589832 | tf_op jit(solution)/shard_map/ppermute | solution.py:268
  18.4 1.3 %collective-permute-start.8 = (bf16[32,5120]{1,0:T(8,128)(2,1)S(1)}, bf16[32,5120]{1,0:T(8,128)(2,1)S(1)}, u32[]{:S(2)}, u32[]{:S(2)}) collective-permute-start(bf16[32,5120]{1,0:T(8,128)(2,1)S(1)} %pad_maximum_fusion), channel_id=1, source_target_pairs={{0,1},{1,0},{2,3},{3,2},{4,6},{5,7},{6,4},{7,5},{8,9},{9,8},{10,11... | collective-permute-start | bytes 983048 | tf_op jit(solution)/shard_map/ppermute | solution.py:268
  19.7 5.8 %collective-permute-done.8 = bf16[32,5120]{1,0:T(8,128)(2,1)S(1)} collective-permute-done((bf16[32,5120]{1,0:T(8,128)(2,1)S(1)}, bf16[32,5120]{1,0:T(8,128)(2,1)S(1)}, u32[]{:S(2)}, u32[]{:S(2)}) %collective-permute-start.8) | collective-permute-done | bytes 327712 | tf_op jit(solution)/shard_map/ppermute | solution.py:268
  25.5 1.1 %collective-permute-start.9 = (bf16[64,5120]{1,0:T(8,128)(2,1)S(1)}, bf16[64,5120]{1,0:T(8,128)(2,1)S(1)}, u32[]{:S(2)}, u32[]{:S(2)}) collective-permute-start(bf16[64,5120]{1,0:T(8,128)(2,1)S(1)} %constant_dynamic-update-slice_fusion.4.refs_0_), channel_id=1, source_target_pairs={{0,2},{1,3},{2,0},{3,1},{4,5},{5,4},{6,7},{7,6},{8,10},{9,11},{10,... | collective-permute-start | bytes 1966088 | tf_op jit(solution)/shard_map/ppermute | solution.py:268
  26.8 0.8 %collective-permute-start.4 = (bf16[64,3072]{1,0:T(8,128)(2,1)S(1)}, bf16[64,3072]{1,0:T(8,128)(2,1)S(1)}, u32[]{:S(2)}, u32[]{:S(2)}) collective-permute-start(bf16[64,3072]{1,0:T(8,128)(2,1)S(1)} %constant_dynamic-update-slice_fusion.refs_0_), channel_id=1, source_target_pairs={{0,8},{1,9},{2,10},{3,11},{4,12},{5,13},{6,14},{7,15},{8,0},{9,1},... | collective-permute-start | bytes 1179656 | tf_op jit(solution)/shard_map/ppermute | solution.py:268
  27.5 8.7 %collective-permute-done.9.refs_0_ = bf16[64,5120]{1,0:T(8,128)(2,1)S(1)} collective-permute-done((bf16[64,5120]{1,0:T(8,128)(2,1)S(1)}, bf16[64,5120]{1,0:T(8,128)(2,1)S(1)}, u32[]{:S(2)}, u32[]{:S(2)}) %collective-permute-start.9) | collective-permute-done | bytes 655392 | tf_op jit(solution)/shard_map/ppermute | solution.py:268
  36.2 0.5 collective-permute-start.11
  36.7 1.6 %collective-permute-done.4.refs_0_ = bf16[64,3072]{1,0:T(8,128)(2,1)S(1)} collective-permute-done((bf16[64,3072]{1,0:T(8,128)(2,1)S(1)}, bf16[64,3072]{1,0:T(8,128)(2,1)S(1)}, u32[]{:S(2)}, u32[]{:S(2)}) %collective-permute-start.4) | collective-permute-done | bytes 393248 | tf_op jit(solution)/shard_map/ppermute | solution.py:268
  38.3 5.8 %load.1.refs_2_.refs_1_ = bf16[16384,512]{1,0:T(8,128)(2,1)S(1)} custom-call(bf16[16384,512]{1,0:T(8,128)(2,1)} %head_ref.1), custom_call_target="tpu_custom_call" | custom-call | bytes 16777216 | tf_op jit(solution)/shard_map/load/pallas_call | solution.py:214
  44.1 2.0 %head.6.refs_3_ = f32[16,8,512]{2,1,0:T(8,128)S(1)} custom-call(bf16[64,5120]{1,0:T(8,128)(2,1)S(1)} %constant_dynamic-update-slice_fusion.4.refs_0_, bf16[64,5120]{1,0:T(8,128)(2,1)S(1)} %collective-permute-done.12.refs_1_, bf16[16384,512]{1,0:T(8,128)(2,1)S(1)} %load.1.refs_2_.refs_1_), custom_call_target="tpu_custom_call" | custom-call | flops 671088640 | bytes 1310720 | tf_op jit(solution)/shard_map/head/pallas_call | solution.py:194
  46.1 1.2 %head.7.refs_2_ = f32[16,8,512]{2,1,0:T(8,128)S(1)} custom-call(bf16[64,3072]{1,0:T(8,128)(2,1)S(1)} %constant_dynamic-update-slice_fusion.refs_0_, bf16[64,3072]{1,0:T(8,128)(2,1)S(1)} %collective-permute-done.11.refs_1_, bf16[16384,512]{1,0:T(8,128)(2,1)S(1)} %load.1.refs_2_.refs_1_, f32[16,8,512]{2,1,0:T(8,128)S(1)} %head.6.refs_3_), custom_call_target="tpu_custom_call", output_to_operand_aliasing={{}: (3, {})} | custom-call | flops 402653184 | bytes 786432 | tf_op jit(solution)/shard_map/head/pallas_call | solution.py:194
  47.4 1.1 %head.8.refs_2_ = f32[16,8,512]{2,1,0:T(8,128)S(1)} custom-call(bf16[64,5120]{1,0:T(8,128)(2,1)S(1)} %collective-permute-done.9.refs_0_, bf16[16384,512]{1,0:T(8,128)(2,1)S(1)} %load.1.refs_2_.refs_1_, f32[16,8,512]{2,1,0:T(8,128)S(1)} %head.7.refs_2_), custom_call_target="tpu_custom_call", output_to_operand_aliasing={{}: (2, {})} | custom-call | flops 335544320 | bytes 655360 | tf_op jit(solution)/shard_map/head/pallas_call | solution.py:194
  48.5 0.7 %head.9.refs_2_ = f32[16,8,512]{2,1,0:T(8,128)S(1)} custom-call(bf16[64,3072]{1,0:T(8,128)(2,1)S(1)} %collective-permute-done.4.refs_0_, bf16[16384,512]{1,0:T(8,128)(2,1)S(1)} %load.1.refs_2_.refs_1_, f32[16,8,512]{2,1,0:T(8,128)S(1)} %head.8.refs_2_), custom_call_target="tpu_custom_call", output_to_operand_aliasing={{}: (2, {})} | custom-call | flops 201326592 | bytes 393216 | tf_op jit(solution)/shard_map/head/pallas_call | solution.py:194
  49.2 1.0 %head.10.refs_2_ = f32[16,8,512]{2,1,0:T(8,128)S(1)} custom-call(bf16[64,5120]{1,0:T(8,128)(2,1)S(1)} %collective-permute-done.10.refs_0_, bf16[16384,512]{1,0:T(8,128)(2,1)S(1)} %load.1.refs_2_.refs_1_, f32[16,8,512]{2,1,0:T(8,128)S(1)} %head.9.refs_2_), custom_call_target="tpu_custom_call", output_to_operand_aliasing={{}: (2, {})} | custom-call | flops 335544320 | bytes 655360 | tf_op jit(solution)/shard_map/head/pallas_call | solution.py:194
  50.2 0.9 %head.11 = f32[32,4,640]{2,1,0:T(4,128)S(1)} custom-call(bf16[64,3072]{1,0:T(8,128)(2,1)S(1)} %collective-permute-done.5.refs_0_, bf16[16384,512]{1,0:T(8,128)(2,1)S(1)} %load.1.refs_2_.refs_1_, f32[16,8,512]{2,1,0:T(8,128)S(1)} %head.10.refs_2_), custom_call_target="tpu_custom_call" | custom-call | flops 201326592 | bytes 393216 | tf_op jit(solution)/shard_map/head/pallas_call | solution.py:194
  51.2 13.9 %all_to_all.5 = f16[32,4,640]{2,1,0:T(4,128)(2,1)S(1)} all-to-all(f16[32,4,640]{2,1,0:T(4,128)(2,1)S(1)} %convert_element_type.6), channel_id=1, replica_groups=mesh['grp'=8,'tp'=4] {'grp','tp'}, dimensions={0} | all-to-all | bytes 327680 | tf_op jit(solution)/shard_map/all_to_all | solution.py:299
  65.2 1.0 %finish.1 = f32[4,16384]{1,0:T(4,128)} custom-call(f32[32,4,640]{2,1,0:T(4,128)S(1)} %convert_element_type.7.got_ref), custom_call_target="tpu_custom_call" | custom-call | tf_op jit(solution)/shard_map/finish/pallas_call | solution.py:240
  (27 shorter events, 1.6 us)
Async XLA Ops:
  0.0 1.7 %collective-permute-start = (bf16[4,16384]{1,0:T(4,128)(2,1)}, bf16[4,16384]{1,0:T(4,128)(2,1)S(1)}, u32[]{:S(2)}, u32[]{:S(2)}) collective-permute-start(bf16[4,16384]{1,0:T(4,128)(2,1)} %hidden_ref.1), channel_id=1, source_target_pairs={{0,4},{1,5},{2,6},{3,7},{4,0},{5,1},{6,2},{7,3},{8,12},{9,13},{10,... | collective-permute-start | bytes 393224 | tf_op jit(solution)/shard_map/ppermute | solution.py:268
  2.0 8.5 %collective-permute-start.6 = (bf16[8,5120]{1,0:T(8,128)(2,1)S(1)}, bf16[8,5120]{1,0:T(8,128)(2,1)S(1)}, u32[]{:S(2)}, u32[]{:S(2)}) collective-permute-start(bf16[8,5120]{1,0:T(8,128)(2,1)S(1)} %get-tuple-element.12), channel_id=1, source_target_pairs={{0,16},{1,17},{2,18},{3,19},{4,20},{5,21},{6,22},{7,23},{8,24},{9,... | collective-permute-start | bytes 245768 | tf_op jit(solution)/shard_map/ppermute | solution.py:268
  6.0 4.1 %collective-permute-start.1 = (bf16[8,3072]{1,0:T(8,128)(2,1)S(1)}, bf16[8,3072]{1,0:T(8,128)(2,1)S(1)}, u32[]{:S(2)}, u32[]{:S(2)}) collective-permute-start(bf16[8,3072]{1,0:T(8,128)(2,1)S(1)} %get-tuple-element.11), channel_id=1, source_target_pairs={{0,1},{1,0},{2,3},{3,2},{4,6},{5,7},{6,4},{7,5},{8,9},{9,8},{10,11... | collective-permute-start | bytes 147464 | tf_op jit(solution)/shard_map/ppermute | solution.py:268
  10.1 6.3 %collective-permute-start.2 = (bf16[16,3072]{1,0:T(8,128)(2,1)S(1)}, bf16[16,3072]{1,0:T(8,128)(2,1)S(1)}, u32[]{:S(2)}, u32[]{:S(2)}) collective-permute-start(bf16[16,3072]{1,0:T(8,128)(2,1)S(1)} %pad_maximum_fusion.3), channel_id=1, source_target_pairs={{0,16},{1,17},{2,18},{3,19},{4,20},{5,21},{6,22},{7,23},{8,24},{9,... | collective-permute-start | bytes 294920 | tf_op jit(solution)/shard_map/ppermute | solution.py:268
  10.6 7.8 %collective-permute-start.7 = (bf16[16,5120]{1,0:T(8,128)(2,1)S(1)}, bf16[16,5120]{1,0:T(8,128)(2,1)S(1)}, u32[]{:S(2)}, u32[]{:S(2)}) collective-permute-start(bf16[16,5120]{1,0:T(8,128)(2,1)S(1)} %pad_maximum_fusion.2), channel_id=1, source_target_pairs={{0,8},{1,9},{2,10},{3,11},{4,12},{5,13},{6,14},{7,15},{8,0},{9,1},... | collective-permute-start | bytes 491528 | tf_op jit(solution)/shard_map/ppermute | solution.py:268
  16.5 10.2 %collective-permute-start.3 = (bf16[32,3072]{1,0:T(8,128)(2,1)S(1)}, bf16[32,3072]{1,0:T(8,128)(2,1)S(1)}, u32[]{:S(2)}, u32[]{:S(2)}) collective-permute-start(bf16[32,3072]{1,0:T(8,128)(2,1)S(1)} %pad_maximum_fusion.1), channel_id=1, source_target_pairs={{0,2},{1,3},{2,0},{3,1},{4,5},{5,4},{6,7},{7,6},{8,10},{9,11},{10,... | collective-permute-start | bytes 589832 | tf_op jit(solution)/shard_map/ppermute | solution.py:268
  18.4 7.1 %collective-permute-start.8 = (bf16[32,5120]{1,0:T(8,128)(2,1)S(1)}, bf16[32,5120]{1,0:T(8,128)(2,1)S(1)}, u32[]{:S(2)}, u32[]{:S(2)}) collective-permute-start(bf16[32,5120]{1,0:T(8,128)(2,1)S(1)} %pad_maximum_fusion), channel_id=1, source_target_pairs={{0,1},{1,0},{2,3},{3,2},{4,6},{5,7},{6,4},{7,5},{8,9},{9,8},{10,11... | collective-permute-start | bytes 983048 | tf_op jit(solution)/shard_map/ppermute | solution.py:268
  25.5 10.7 %collective-permute-start.9 = (bf16[64,5120]{1,0:T(8,128)(2,1)S(1)}, bf16[64,5120]{1,0:T(8,128)(2,1)S(1)}, u32[]{:S(2)}, u32[]{:S(2)}) collective-permute-start(bf16[64,5120]{1,0:T(8,128)(2,1)S(1)} %constant_dynamic-update-slice_fusion.4.refs_0_), channel_id=1, source_target_pairs={{0,2},{1,3},{2,0},{3,1},{4,5},{5,4},{6,7},{7,6},{8,10},{9,11},{10,... | collective-permute-start | bytes 1966088 | tf_op jit(solution)/shard_map/ppermute | solution.py:268
  26.6 17.5 %collective-permute-start.12 = (bf16[64,5120]{1,0:T(8,128)(2,1)S(1)}, bf16[64,5120]{1,0:T(8,128)(2,1)S(1)}, u32[]{:S(2)}, u32[]{:S(2)}) collective-permute-start(bf16[64,5120]{1,0:T(8,128)(2,1)S(1)} %constant_dynamic-update-slice_fusion.4.refs_0_), channel_id=1, source_target_pairs={{0,4},{1,5},{2,6},{3,7},{4,0},{5,1},{6,2},{7,3},{8,12},{9,13},{10,... | collective-permute-start | bytes 1966088 | tf_op jit(solution)/shard_map/ppermute | solution.py:268
  26.8 11.6 %collective-permute-start.4 = (bf16[64,3072]{1,0:T(8,128)(2,1)S(1)}, bf16[64,3072]{1,0:T(8,128)(2,1)S(1)}, u32[]{:S(2)}, u32[]{:S(2)}) collective-permute-start(bf16[64,3072]{1,0:T(8,128)(2,1)S(1)} %constant_dynamic-update-slice_fusion.refs_0_), channel_id=1, source_target_pairs={{0,8},{1,9},{2,10},{3,11},{4,12},{5,13},{6,14},{7,15},{8,0},{9,1},... | collective-permute-start | bytes 1179656 | tf_op jit(solution)/shard_map/ppermute | solution.py:268
  36.2 13.0 %collective-permute-start.10 = (bf16[64,5120]{1,0:T(8,128)(2,1)S(1)}, bf16[64,5120]{1,0:T(8,128)(2,1)S(1)}, u32[]{:S(2)}, u32[]{:S(2)}) collective-permute-start(bf16[64,5120]{1,0:T(8,128)(2,1)S(1)} %collective-permute-done.9.refs_0_), channel_id=1, source_target_pairs={{0,4},{1,5},{2,6},{3,7},{4,0},{5,1},{6,2},{7,3},{8,12},{9,13},{10,... | collective-permute-start | bytes 1966088 | tf_op jit(solution)/shard_map/ppermute | solution.py:268
  36.2 10.0 %collective-permute-start.11 = (bf16[64,3072]{1,0:T(8,128)(2,1)S(1)}, bf16[64,3072]{1,0:T(8,128)(2,1)S(1)}, u32[]{:S(2)}, u32[]{:S(2)}) collective-permute-start(bf16[64,3072]{1,0:T(8,128)(2,1)S(1)} %constant_dynamic-update-slice_fusion.refs_0_), channel_id=1, source_target_pairs={{0,4},{1,5},{2,6},{3,7},{4,0},{5,1},{6,2},{7,3},{8,12},{9,13},{10,... | collective-permute-start | bytes 1179656 | tf_op jit(solution)/shard_map/ppermute | solution.py:268
  38.3 11.9 %collective-permute-start.5 = (bf16[64,3072]{1,0:T(8,128)(2,1)S(1)}, bf16[64,3072]{1,0:T(8,128)(2,1)S(1)}, u32[]{:S(2)}, u32[]{:S(2)}) collective-permute-start(bf16[64,3072]{1,0:T(8,128)(2,1)S(1)} %collective-permute-done.4.refs_0_), channel_id=1, source_target_pairs={{0,4},{1,5},{2,6},{3,7},{4,0},{5,1},{6,2},{7,3},{8,12},{9,13},{10,... | collective-permute-start | bytes 1179656 | tf_op jit(solution)/shard_map/ppermute | solution.py:268
